TPU v7x, 32 devices: a whole 2x2x4 slice. The times are simulated.
32 devices in a mesh: section: 4 (over y, x), tensor: 8 (over z, core).
Axes of the slice: x: 2, y: 2, z: 4, core: 2. Of those that a mesh axis runs over, the one named last changes fastest.
Arguments:
- hidden_last: bfloat16 [512, 6656], P(None, 'tensor'), may hold values from -6 to 6
- labels: int32 [512], replicated, may hold values from 0 to 31999
- head_weight: bfloat16 [6656, 32000], P(None, 'tensor'), may hold values from -0.21875 to 0.21875
- layer_inputs: bfloat16 [4, 512, 6656], P('section', None, 'tensor'), may hold values from -6 to 6
- weights: bfloat16 [4, 6656, 6656], P('section', 'tensor'), may hold values from -0.078125 to 0.078125
- row_state: float32 [4, 6656], P('section', 'tensor'), may hold values from 1.173753e-06 to 0.000498845
- col_state: float32 [4, 6656], P('section'), may hold values from 1e-08 to 1e-06
Outputs:
- loss: float32 [], replicated
- input_grads: bfloat16 [4, 512, 6656], P('section', None, 'tensor')
- new_weights: bfloat16 [4, 6656, 6656], P('section', 'tensor')
- new_row_state: float32 [4, 6656], P('section', 'tensor')
- new_col_state: float32 [4, 6656], P('section')
All inputs are finite; a program needn't handle non-finite values.
Results may differ from a plain program's by a relative error of at most 0.007.
Values may be sent and summed in bfloat16 or wider, within the bound.
A program may use at most 192 MiB of HBM per device.

v0:
```python
import jax
import jax.numpy as jnp
from jax import lax
from jax.sharding import PartitionSpec as P

decay_rate = 0.9
learn_rate = 0.3
tiny_term = 1e-30


def shifted(block, axis, distance):
    devices = range(lax.axis_size(axis))
    route = [(i - distance, i) for i in devices if i - distance in devices]
    return lax.ppermute(block, axis, route)


def body(hidden_last, labels, head_weight, layer_inputs, weights, row_state, col_state):
    section_count = lax.axis_size("section")
    section_index = lax.axis_index("section")
    all_rows = labels.shape[0]
    model_width = head_weight.shape[0]
    vocab_local = head_weight.shape[1]
    local_weight = weights[0]
    rows_local = local_weight.shape[0]
    saved_all = layer_inputs[0]
    columns = lax.axis_index("tensor") * vocab_local + lax.iota(jnp.int32, vocab_local)
    share_rows = all_rows // section_count
    row_start = section_index * share_rows
    hidden_rows = lax.dynamic_slice_in_dim(hidden_last, row_start, share_rows, 0)
    head_slice = head_weight
    logits = jnp.dot(
        lax.all_gather(hidden_rows, "tensor", axis=1, tiled=True),
        head_slice,
        preferred_element_type=jnp.float32,
    )
    exponent = jnp.exp(logits)
    label_hit = (
        lax.dynamic_slice_in_dim(labels, row_start, share_rows, 0)[:, None] == columns[None, :]
    )
    denominator, picked = lax.psum(
        (
            jnp.sum(exponent, axis=1),
            jnp.sum(jnp.where(label_hit, logits, jnp.zeros_like(logits)), axis=1),
        ),
        "tensor",
    )
    losses = jnp.log(denominator) - picked
    logit_grad = (
        (exponent / denominator[:, None] - label_hit.astype(jnp.float32)) / all_rows
    ).astype(jnp.bfloat16)
    head_slice = head_weight
    shares = lax.psum_scatter(
        lax.dot_general(
            head_slice, logit_grad, (((1,), (1,)), ((), ())), preferred_element_type=jnp.float32
        ),
        "tensor",
        scatter_dimension=0,
        tiled=True,
    )
    part_grad = shares.T.astype(jnp.bfloat16)
    part_loss = jnp.sum(losses)
    head_grad = lax.all_gather(part_grad, "section", axis=0, tiled=True)
    loss = lax.psum(part_loss, "section") / all_rows
    is_last = section_index == section_count - 1

    def layer_block(dy_rows, saved_rows):
        gathered = lax.all_gather(dy_rows, "tensor", axis=1, tiled=True)
        backward = lax.dot_general(
            gathered, local_weight, (((1,), (1,)), ((), ())), preferred_element_type=jnp.float32
        )
        product = lax.dot_general(
            saved_rows, gathered, (((0,), (0,)), ((), ())), preferred_element_type=jnp.float32
        )
        backward, piece_grad = (backward, product)
        input_grad = (dy_rows.astype(jnp.float32) + backward).astype(jnp.bfloat16)
        return (input_grad, piece_grad)

    start_grad = jnp.zeros((rows_local, model_width), jnp.float32)

    def advance_whole(step_index, loop_state):
        received, gradient, outputs = loop_state
        active = step_index == section_count - 1 - section_index
        dy_rows = jnp.where(is_last, head_grad, received)
        input_grad, piece_grad = layer_block(dy_rows, saved_all)
        gradient = gradient + jnp.where(active, piece_grad, jnp.zeros_like(piece_grad))
        outputs = jnp.where(active, input_grad, outputs)
        received = shifted(input_grad, "section", -1)
        return (received, gradient, outputs)

    loop_state = (
        jnp.zeros((all_rows, rows_local), jnp.bfloat16),
        start_grad,
        jnp.zeros((all_rows, rows_local), jnp.bfloat16),
    )
    loop_state = lax.fori_loop(0, section_count, advance_whole, loop_state)
    gradient = loop_state[1]
    outputs = loop_state[2]
    weight_float = local_weight.astype(jnp.float32)
    squares = gradient * gradient + tiny_term
    row_new = decay_rate * row_state[0] + (1.0 - decay_rate) * jnp.mean(squares, axis=1)
    col_part = jnp.sum(squares, axis=0)
    entries = float(model_width * model_width)
    col_sum, row_total, weight_total = lax.psum(
        (col_part, jnp.sum(row_new), jnp.sum(weight_float * weight_float)), "tensor"
    )
    col_new = decay_rate * col_state[0] + (1.0 - decay_rate) * (col_sum / model_width)
    update = gradient / jnp.sqrt(row_new[:, None] * col_new[None, :] / row_total)
    update_total = lax.psum(jnp.sum(update * update), "tensor")
    factor = (
        learn_rate
        * jnp.sqrt(weight_total / entries)
        / jnp.maximum(1.0, jnp.sqrt(update_total / entries))
    )
    new_weight = (weight_float - factor * update).astype(jnp.bfloat16)
    return (loss, outputs[None], new_weight[None], row_new[None], col_new[None])


def solution(mesh):
    return jax.shard_map(
        body,
        mesh=mesh,
        in_specs=(
            P(None, "tensor"),
            P(),
            P(None, "tensor"),
            P("section", None, "tensor"),
            P("section", "tensor", None),
            P("section", "tensor"),
            P("section", None),
        ),
        out_specs=(
            P(),
            P("section", None, "tensor"),
            P("section", "tensor", None),
            P("section", "tensor"),
            P("section", None),
        ),
        check_vma=False,
    )
```

profile of v0, /device:TPU:0, one launch (start us, length us, event | category | flops | bytes accessed | tf_op | source)
XLA Modules:
  0.0 680.5 jit_solution(17623979021237377767)
XLA Ops:
  7.2 1.1 copy-done
  8.3 0.7 constant_dynamic-slice_fusion
  9.1 0.8 dynamic_slice.7
  9.9 29.1 %all-gather.3.cloned.1.call-done = bf16[128,6656]{0,1:T(8,128)(2,1)} async-done(((bf16[128,832]{0,1:T(8,128)(2,1)}), bf16[128,6656]{0,1:T(8,128)(2,1)}) %all-gather.3.cloned.1.call-update) | async-done | bytes 1703952 | tf_op jit(solution)/shard_map/all_gather | solution.py:32
  39.0 22.1 %exponential_reduce_fusion = (f32[128]{0:T(128)S(1)}, f32[128]{0:T(128)}, f32[128,4000]{0,1:T(8,128)S(1)}) fusion(s32[4000]{0:T(1024)S(1)} %iota_add_fusion, s32[128]{0:T(128)S(1)} %dynamic_slice.7, bf16[6656,4000]{0,1:T(8,128)(2,1)} %param.11, bf16[128,6656]{0,1:T(8,128)(2,1)} %all-gather.3.cloned.1.call-done), kind=kOutput, calls=%fused_computation.21 | convolution fusion | flops 6817792000 | bytes 57017472 | tf_op jit(solution)/shard_map/dot_general | solution.py:31
  61.0 15.1 %psum.49 = f32[128]{0:T(128)S(1)} all-reduce(f32[128]{0:T(128)S(1)} %get-tuple-element.270), channel_id=1, replica_groups=mesh['section'=4,'tensor'=8] {'tensor'}, use_global_device_ids=true, to_apply=%region_1.2 | all-reduce | flops 128 | bytes 1024 | tf_op jit(solution)/shard_map/psum | solution.py:40
  76.2 20.9 %convolution_bitcast_fusion = f32[6656,128]{0,1:T(8,128)} fusion(bf16[6656,4000]{0,1:T(8,128)(2,1)} %param.11, f32[128,4000]{0,1:T(8,128)S(1)} %get-tuple-element.300, f32[128]{0:T(128)S(1)} %psum.49, s32[128]{0:T(128)S(1)} %dynamic_slice.7, s32[4000]{0:T(1024)S(1)} %iota_add_fusion), kind=kOutput, calls=%fused_computation.14 | convolution fusion | flops 6818816000 | bytes 58720896 | tf_op jit(solution)/shard_map/dot_general | solution.py:53
  97.1 5.1 copy.16
  102.8 0.6 multiply_reduce_fusion.2
  103.4 0.7 multiply_reduce_fusion.1
  104.1 10.8 %fusion = f32[]{:T(128)} fusion(bf16[1,832,6656]{2,1,0:T(8,128)(2,1)} %param.13), kind=kLoop, calls=%fused_computation.6 | loop fusion | flops 16613375 | bytes 11075588 | tf_op jit(solution)/shard_map/reduce_sum | solution.py:104
  114.9 28.1 %reduce-scatter.4.cloned.1.call-done = f32[832,128]{1,0:T(8,128)} async-done(((f32[6656,128]{1,0:T(8,128)}), f32[832,128]{1,0:T(8,128)}) %reduce-scatter.4.cloned.1.call-update) | async-done | bytes 426000
  142.9 1.2 copy.17
  144.1 12.6 %all_gather.16 = bf16[512,832]{1,0:T(8,128)(2,1)S(1)} all-gather(bf16[128,832]{1,0:T(8,128)(2,1)S(1)} %bitcast.35), channel_id=1, replica_groups=mesh['section'=4,'tensor'=8] {'section'}, dimensions={0}, use_global_device_ids=true | all-gather | bytes 1064960 | tf_op jit(solution)/shard_map/all_gather | solution.py:62
  157.3 420.9 %while.20 = (s32[]{:T(128)}, bf16[512,832]{0,1:T(8,128)(2,1)S(1)}, f32[832,6656]{1,0:T(8,128)}, bf16[512,832]{0,1:T(8,128)(2,1)}, pred[]{:T(512)}, /*index=5*/bf...) while((s32[]{:T(128)}, bf16[512,832]{0,1:T(8,128)(2,1)S(1)}, ...), condition=%wide.region_8.9_spmd.clone, body=%wide.region_7.8_spmd.clone.sunk | while | flops 11360567296 | bytes 102236368 | solution.py:95
  157.4 1.0 broadcast_select_fusion.2
  158.4 70.2 %all-gather.5.cloned.1.call-done = bf16[512,6656]{0,1:T(8,128)(2,1)} async-done(((bf16[512,832]{0,1:T(8,128)(2,1)}), bf16[512,6656]{0,1:T(8,128)(2,1)}) %all-gather.5.cloned.1.call-update) | async-done | bytes 6815760 | tf_op jit(solution)/shard_map/while/body/eval_jaxpr/all_gather | solution.py:67
  228.6 11.6 %select_select_fusion.2 = (bf16[512,832]{0,1:T(8,128)(2,1)}, bf16[512,832]{0,1:T(8,128)(2,1)S(1)}) fusion(bf16[512,832]{0,1:T(8,128)(2,1)} %get-tuple-element.374, pred[]{:T(512)S(6)} %compare.3, pred[]{:T(512)S(6)} %eq.52, bf16[832,6656]{1,0:T(8,128)(2,1)} %get-tuple-element.388, bf16[512,6656]{0,1:T(8,128)(2,1)} %all-gather.5.cloned.1.call-done, ...), kind=kOutput, calls=%fused_computation.2.clone.1 | convolution fusion | flops 5672828928 | bytes 21299202 | tf_op jit(solution)/shard_map/while/body/eval_jaxpr/dot_general | solution.py:68
  240.1 1.3 collective-permute-start
  241.4 12.6 %bitcast_add_fusion.2 = f32[832,6656]{1,0:T(8,128)} fusion(f32[832,6656]{1,0:T(8,128)} %get-tuple-element.373, bf16[512,6656]{0,1:T(8,128)(2,1)} %all-gather.5.cloned.1.call-done, bf16[512,832]{1,0:T(8,128)(2,1)S(1)} %get-tuple-element.390, pred[]{:T(512)S(6)} %compare.3, pred[]{:T(512)S(6)} %eq.52), kind=kOutput, calls=%fused_computation.clone.1 | convolution fusion | flops 5687312384 | bytes 51970048 | tf_op jit(solution)/shard_map/while/body/eval_jaxpr/dot_general | solution.py:71
  254.1 9.1 %collective-permute-done = bf16[512,832]{0,1:T(8,128)(2,1)S(1)} collective-permute-done((bf16[512,832]{0,1:T(8,128)(2,1)S(1)}, bf16[512,832]{0,1:T(8,128)(2,1)S(1)}, u32[]{:S(2)}, u32[]{:S(2)}) %collective-permute-start) | collective-permute-done | bytes 852000 | tf_op jit(solution)/shard_map/while/body/eval_jaxpr/ppermute | solution.py:14
  263.1 1.0 broadcast_select_fusion.2
  264.1 69.3 %all-gather.5.cloned.1.call-done = bf16[512,6656]{0,1:T(8,128)(2,1)} async-done(((bf16[512,832]{0,1:T(8,128)(2,1)}), bf16[512,6656]{0,1:T(8,128)(2,1)}) %all-gather.5.cloned.1.call-update) | async-done | bytes 6815760 | tf_op jit(solution)/shard_map/while/body/eval_jaxpr/all_gather | solution.py:67
  333.5 11.7 %select_select_fusion.2 = (bf16[512,832]{0,1:T(8,128)(2,1)}, bf16[512,832]{0,1:T(8,128)(2,1)S(1)}) fusion(bf16[512,832]{0,1:T(8,128)(2,1)} %get-tuple-element.374, pred[]{:T(512)S(6)} %compare.3, pred[]{:T(512)S(6)} %eq.52, bf16[832,6656]{1,0:T(8,128)(2,1)} %get-tuple-element.388, bf16[512,6656]{0,1:T(8,128)(2,1)} %all-gather.5.cloned.1.call-done, ...), kind=kOutput, calls=%fused_computation.2.clone.1 | convolution fusion | flops 5672828928 | bytes 21299202 | tf_op jit(solution)/shard_map/while/body/eval_jaxpr/dot_general | solution.py:68
  345.2 1.3 collective-permute-start
  346.5 16.7 %bitcast_add_fusion.2 = f32[832,6656]{1,0:T(8,128)} fusion(f32[832,6656]{1,0:T(8,128)} %get-tuple-element.373, bf16[512,6656]{0,1:T(8,128)(2,1)} %all-gather.5.cloned.1.call-done, bf16[512,832]{1,0:T(8,128)(2,1)S(1)} %get-tuple-element.390, pred[]{:T(512)S(6)} %compare.3, pred[]{:T(512)S(6)} %eq.52), kind=kOutput, calls=%fused_computation.clone.1 | convolution fusion | flops 5687312384 | bytes 51970048 | tf_op jit(solution)/shard_map/while/body/eval_jaxpr/dot_general | solution.py:71
  363.1 5.0 collective-permute-done
  368.2 1.0 broadcast_select_fusion.2
  369.2 69.3 %all-gather.5.cloned.1.call-done = bf16[512,6656]{0,1:T(8,128)(2,1)} async-done(((bf16[512,832]{0,1:T(8,128)(2,1)}), bf16[512,6656]{0,1:T(8,128)(2,1)}) %all-gather.5.cloned.1.call-update) | async-done | bytes 6815760 | tf_op jit(solution)/shard_map/while/body/eval_jaxpr/all_gather | solution.py:67
  438.5 11.7 %select_select_fusion.2 = (bf16[512,832]{0,1:T(8,128)(2,1)}, bf16[512,832]{0,1:T(8,128)(2,1)S(1)}) fusion(bf16[512,832]{0,1:T(8,128)(2,1)} %get-tuple-element.374, pred[]{:T(512)S(6)} %compare.3, pred[]{:T(512)S(6)} %eq.52, bf16[832,6656]{1,0:T(8,128)(2,1)} %get-tuple-element.388, bf16[512,6656]{0,1:T(8,128)(2,1)} %all-gather.5.cloned.1.call-done, ...), kind=kOutput, calls=%fused_computation.2.clone.1 | convolution fusion | flops 5672828928 | bytes 21299202 | tf_op jit(solution)/shard_map/while/body/eval_jaxpr/dot_general | solution.py:68
  450.2 1.3 collective-permute-start
  451.5 16.7 %bitcast_add_fusion.2 = f32[832,6656]{1,0:T(8,128)} fusion(f32[832,6656]{1,0:T(8,128)} %get-tuple-element.373, bf16[512,6656]{0,1:T(8,128)(2,1)} %all-gather.5.cloned.1.call-done, bf16[512,832]{1,0:T(8,128)(2,1)S(1)} %get-tuple-element.390, pred[]{:T(512)S(6)} %compare.3, pred[]{:T(512)S(6)} %eq.52), kind=kOutput, calls=%fused_computation.clone.1 | convolution fusion | flops 5687312384 | bytes 51970048 | tf_op jit(solution)/shard_map/while/body/eval_jaxpr/dot_general | solution.py:71
  468.2 5.0 collective-permute-done
  473.2 1.0 broadcast_select_fusion.2
  474.2 69.3 %all-gather.5.cloned.1.call-done = bf16[512,6656]{0,1:T(8,128)(2,1)} async-done(((bf16[512,832]{0,1:T(8,128)(2,1)}), bf16[512,6656]{0,1:T(8,128)(2,1)}) %all-gather.5.cloned.1.call-update) | async-done | bytes 6815760 | tf_op jit(solution)/shard_map/while/body/eval_jaxpr/all_gather | solution.py:67
  543.6 11.7 %select_select_fusion.2 = (bf16[512,832]{0,1:T(8,128)(2,1)}, bf16[512,832]{0,1:T(8,128)(2,1)S(1)}) fusion(bf16[512,832]{0,1:T(8,128)(2,1)} %get-tuple-element.374, pred[]{:T(512)S(6)} %compare.3, pred[]{:T(512)S(6)} %eq.52, bf16[832,6656]{1,0:T(8,128)(2,1)} %get-tuple-element.388, bf16[512,6656]{0,1:T(8,128)(2,1)} %all-gather.5.cloned.1.call-done, ...), kind=kOutput, calls=%fused_computation.2.clone.1 | convolution fusion | flops 5672828928 | bytes 21299202 | tf_op jit(solution)/shard_map/while/body/eval_jaxpr/dot_general | solution.py:68
  555.3 1.3 collective-permute-start
  556.6 16.7 %bitcast_add_fusion.2 = f32[832,6656]{1,0:T(8,128)} fusion(f32[832,6656]{1,0:T(8,128)} %get-tuple-element.373, bf16[512,6656]{0,1:T(8,128)(2,1)} %all-gather.5.cloned.1.call-done, bf16[512,832]{1,0:T(8,128)(2,1)S(1)} %get-tuple-element.390, pred[]{:T(512)S(6)} %compare.3, pred[]{:T(512)S(6)} %eq.52), kind=kOutput, calls=%fused_computation.clone.1 | convolution fusion | flops 5687312384 | bytes 51970048 | tf_op jit(solution)/shard_map/while/body/eval_jaxpr/dot_general | solution.py:71
  573.2 5.0 collective-permute-done
  578.3 9.7 %fusion.2 = (f32[6656]{0:T(1024)S(1)}, f32[832]{0:T(1024)S(1)}) fusion(f32[832,6656]{1,0:T(8,128)} %get-tuple-element.219), kind=kLoop, calls=%fused_computation.11 | loop fusion | flops 22143680 | bytes 22181120 | tf_op jit(solution)/shard_map/reduce_sum | solution.py:101
  588.0 0.6 fusion.16
  588.6 26.0 %all-reduce.1 = (f32[]{:T(128)}, f32[6656]{0:T(1024)S(1)}) all-reduce(f32[]{:T(128)} %get-tuple-element.295, f32[6656]{0:T(1024)S(1)} %get-tuple-element.268), channel_id=1, replica_groups=mesh['section'=4,'tensor'=8] {'tensor'}, use_global_device_ids=true, to_apply=%region_15.16 | all-reduce | flops 6657 | bytes 53256 | tf_op jit(solution)/shard_map/psum | solution.py:103
  614.6 11.9 %multiply_reduce_fusion = f32[]{:T(128)} fusion(f32[832,6656]{1,0:T(8,128)} %get-tuple-element.219, f32[]{:T(128)} %get-tuple-element.293, f32[6656]{0:T(1024)S(1)} %multiply_add_fusion.1, f32[832]{0:T(1024)S(1)} %get-tuple-element.296), kind=kLoop, calls=%fused_computation.8 | loop fusion | flops 27688960 | bytes 22181128 | tf_op jit(solution)/shard_map/reduce_sum | solution.py:108
  626.5 14.2 %all-reduce = (f32[128]{0:T(128)S(1)}, f32[]{:T(128)}, f32[]{:T(128)}) all-reduce(f32[128]{0:T(128)S(1)} %copy-done.10, f32[]{:T(128)} %fusion, f32[]{:T(128)} %multiply_reduce_fusion), channel_id=1, replica_groups=mesh['section'=4,'tensor'=8] {'tensor'}, use_global_device_ids=true, to_apply=%region_3.4 | all-reduce | flops 130 | bytes 1040 | tf_op jit(solution)/shard_map/psum | solution.py:40
  642.2 17.4 %fusion.4 = bf16[1,832,6656]{2,1,0:T(8,128)(2,1)} fusion(f32[]{:T(128)S(6)} %div.49, bf16[1,832,6656]{2,1,0:T(8,128)(2,1)} %bitcast.33, f32[832,6656]{1,0:T(8,128)} %get-tuple-element.219, f32[]{:T(128)} %get-tuple-element.293, f32[6656]{0:T(1024)S(1)} %multiply_add_fusion.1, f32[832]{0:T(1024)S(1)} %get-tuple-element.296), kind=kLoop, calls=%fused_computation.13 | loop fusion | flops 38764544 | bytes 44332296 | tf_op jit(solution)/shard_map/broadcast_in_dim | solution.py:115
  659.6 0.6 subtract_reduce_fusion
  660.2 0.6 broadcast_in_dim.21
  660.8 10.4 %psum.51 = f32[]{:T(128)} all-reduce(f32[]{:T(128)} %subtract_reduce_fusion), channel_id=1, replica_groups=mesh['section'=4,'tensor'=8] {'section'}, use_global_device_ids=true, to_apply=%region_5.6 | all-reduce | flops 1 | bytes 8 | tf_op jit(solution)/shard_map/psum | solution.py:63
  (41 shorter events, 2.0 us)
Async XLA Ops:
  7.2 1.2 copy-start
  7.2 31.8 %all-gather.3.cloned.1.call-start = ((), (), s32[]{:S(2)}) async-start(), calls=%async_computation.1 | async-start | bytes 1916928 | tf_op jit(solution)/shard_map/all_gather | solution.py:32
  9.1 133.9 %reduce-scatter.4.cloned.1.call-start = ((), (), s32[]{:S(2)}) async-start(), calls=%async_computation.2 | async-start | bytes 3833856
  76.2 20.9 %copy-start.8 = (f32[128]{0:T(128)}, f32[128]{0:T(128)S(1)}, u32[]{:S(2)}) copy-start(f32[128]{0:T(128)S(1)} %psum.49) | copy-start | bytes 1540
  76.2 26.0 %copy-start.2 = (bf16[1,512,832]{1,2,0:T(8,128)(2,1)S(1)}, bf16[1,512,832]{1,2,0:T(8,128)(2,1)}, u32[]{:S(2)}) copy-start(bf16[1,512,832]{1,2,0:T(8,128)(2,1)} %param.12) | copy-start | bytes 2555908
  76.2 26.6 %copy-start.6 = (f32[1,832]{1,0:T(1,128)S(1)}, f32[1,832]{1,0:T(1,128)}, u32[]{:S(2)}) copy-start(f32[1,832]{1,0:T(1,128)} %param.14) | copy-start | bytes 9988
  76.2 27.2 %copy-start.4 = (f32[1,6656]{1,0:T(1,128)S(1)}, f32[1,6656]{1,0:T(1,128)}, u32[]{:S(2)}) copy-start(f32[1,6656]{1,0:T(1,128)} %param.15) | copy-start | bytes 79876
  157.3 71.2 %all-gather.5.cloned.1.call-start = ((), (), s32[]{:S(2)}) async-start(), calls=%async_computation.3 | async-start | bytes 7667712 | tf_op jit(solution)/shard_map/while/body/eval_jaxpr/all_gather | solution.py:67
  240.1 23.0 %collective-permute-start = (bf16[512,832]{0,1:T(8,128)(2,1)S(1)}, bf16[512,832]{0,1:T(8,128)(2,1)S(1)}, u32[]{:S(2)}, u32[]{:S(2)}) collective-permute-start(bf16[512,832]{0,1:T(8,128)(2,1)S(1)} %get-tuple-element.358), channel_id=1, source_target_pairs={{8,0},{16,8},{24,16},{9,1},{17,9},{25,17},{10,2},{18,10},{26,18},{... | collective-permute-start | bytes 2555912 | tf_op jit(solution)/shard_map/while/body/eval_jaxpr/ppermute | solution.py:14
  263.1 70.4 %all-gather.5.cloned.1.call-start = ((), (), s32[]{:S(2)}) async-start(), calls=%async_computation.3 | async-start | bytes 7667712 | tf_op jit(solution)/shard_map/while/body/eval_jaxpr/all_gather | solution.py:67
  345.2 23.0 %collective-permute-start = (bf16[512,832]{0,1:T(8,128)(2,1)S(1)}, bf16[512,832]{0,1:T(8,128)(2,1)S(1)}, u32[]{:S(2)}, u32[]{:S(2)}) collective-permute-start(bf16[512,832]{0,1:T(8,128)(2,1)S(1)} %get-tuple-element.358), channel_id=1, source_target_pairs={{8,0},{16,8},{24,16},{9,1},{17,9},{25,17},{10,2},{18,10},{26,18},{... | collective-permute-start | bytes 2555912 | tf_op jit(solution)/shard_map/while/body/eval_jaxpr/ppermute | solution.py:14
  368.2 70.4 %all-gather.5.cloned.1.call-start = ((), (), s32[]{:S(2)}) async-start(), calls=%async_computation.3 | async-start | bytes 7667712 | tf_op jit(solution)/shard_map/while/body/eval_jaxpr/all_gather | solution.py:67
  450.2 23.0 %collective-permute-start = (bf16[512,832]{0,1:T(8,128)(2,1)S(1)}, bf16[512,832]{0,1:T(8,128)(2,1)S(1)}, u32[]{:S(2)}, u32[]{:S(2)}) collective-permute-start(bf16[512,832]{0,1:T(8,128)(2,1)S(1)} %get-tuple-element.358), channel_id=1, source_target_pairs={{8,0},{16,8},{24,16},{9,1},{17,9},{25,17},{10,2},{18,10},{26,18},{... | collective-permute-start | bytes 2555912 | tf_op jit(solution)/shard_map/while/body/eval_jaxpr/ppermute | solution.py:14
  473.2 70.4 %all-gather.5.cloned.1.call-start = ((), (), s32[]{:S(2)}) async-start(), calls=%async_computation.3 | async-start | bytes 7667712 | tf_op jit(solution)/shard_map/while/body/eval_jaxpr/all_gather | solution.py:67
  555.3 23.0 %collective-permute-start = (bf16[512,832]{0,1:T(8,128)(2,1)S(1)}, bf16[512,832]{0,1:T(8,128)(2,1)S(1)}, u32[]{:S(2)}, u32[]{:S(2)}) collective-permute-start(bf16[512,832]{0,1:T(8,128)(2,1)S(1)} %get-tuple-element.358), channel_id=1, source_target_pairs={{8,0},{16,8},{24,16},{9,1},{17,9},{25,17},{10,2},{18,10},{26,18},{... | collective-permute-start | bytes 2555912 | tf_op jit(solution)/shard_map/while/body/eval_jaxpr/ppermute | solution.py:14
  578.2 9.7 %copy-start.5 = (f32[832]{0:T(1024)S(1)}, f32[832]{0:T(1024)}, u32[]{:S(2)}) copy-start(f32[832]{0:T(1024)} %multiply_reduce_fusion.2) | copy-start | bytes 9988
  578.2 36.4 %copy-start.3 = (f32[6656]{0:T(1024)S(1)}, f32[6656]{0:T(1024)}, u32[]{:S(2)}) copy-start(f32[6656]{0:T(1024)} %multiply_reduce_fusion.1) | copy-start | bytes 79876
  578.3 48.3 %copy-start.10 = (f32[128]{0:T(128)S(1)}, f32[128]{0:T(128)}, u32[]{:S(2)}) copy-start(f32[128]{0:T(128)} %get-tuple-element.271) | copy-start | bytes 1540
  642.1 30.4 %copy-start.1 = (bf16[512,832]{0,1:T(8,128)(2,1)S(1)}, bf16[512,832]{0,1:T(8,128)(2,1)}, u32[]{:S(2)}) copy-start(bf16[512,832]{0,1:T(8,128)(2,1)} %param.9) | copy-start | bytes 2555908
  642.2 17.4 %copy-start.9 = (f32[128]{0:T(128)S(1)}, f32[128]{0:T(128)}, u32[]{:S(2)}) copy-start(f32[128]{0:T(128)} %copy-done.8) | copy-start | bytes 1540
  642.2 29.1 %copy-start.7 = (f32[1,832]{1,0:T(1,128)S(1)}, f32[1,832]{1,0:T(1,128)}, u32[]{:S(2)}) copy-start(f32[1,832]{1,0:T(1,128)} %param.14) | copy-start | bytes 9988
Sparse Core Ops, SparseCore 0:
  10.2 28.7 all-gather.2
  102.3 40.6 reduce-scatter.3
  160.3 68.1 all-gather.4
  265.8 67.6 all-gather.4
  370.9 67.6 all-gather.4
  475.9 67.6 all-gather.4
where the time goes:
time: 681 us
  waiting for transfers between devices  360 us (53%)
  matrix products  152 us (22%)
  blocking collectives  78.4 us (12%)
  other arithmetic  56.9 us (8%)
  between operations  17.4 us (3%)
  local copies, waits for them, and re-layouts  10.6 us (2%)
    all_gather x4, waiting for transfers between devices, layer_block(): gathered = lax.all_gather(dy_rows, 'tensor', axis=1, tiled=True)  278 us
    dot_general x4, matrix products, layer_block(): lax.dot_general(saved_rows, gathered, (((0,), (0,)), ((), ())), preferred...  62.6 us
    dot_general x4, matrix products, layer_block(): lax.dot_general(gathered, local_weight, (((1,), (1,)), ((), ())), preferr...  46.7 us
    psum x2, blocking collectives, body(): lax.psum((jnp.sum(exponent, axis=1), jnp.sum(jnp.where(label_hit, logits,...  29.4 us
    all_gather x1, waiting for transfers between devices, body(): lax.all_gather(hidden_rows, 'tensor', axis=1, tiled=True)  29.1 us
    unnamed x3, waiting for transfers between devices  28.1 us
    psum x1, blocking collectives, body(): lax.psum((col_part, jnp.sum(row_new), jnp.sum(weight_float * weight_float...  26 us
    ppermute x4, waiting for transfers between devices, shifted(): return lax.ppermute(block, axis, route)  24.1 us
  transfers between devices with their start and end apart: 10, of which 10 were waited for; matrix products, arithmetic and copies ran while one was open for 11% of the time, Pallas kernels for 0%

commit v1 on v0

--- a/solution.py
+++ b/solution.py
@@ -64,7 +64,16 @@
     is_last = section_index == section_count - 1
 
     def layer_block(dy_rows, saved_rows):
-        gathered = lax.all_gather(dy_rows, "tensor", axis=1, tiled=True)
+        ring = [dy_rows]
+        for hop in range(7):
+            ring.append(
+                lax.ppermute(ring[-1], "tensor", [(dev, (dev + 1) % 8) for dev in range(8)])
+            )
+        gathered = jnp.roll(
+            jnp.concatenate(ring[::-1], axis=1),
+            (lax.axis_index("tensor") + 1) * ring[0].shape[1],
+            axis=1,
+        )
         backward = lax.dot_general(
             gathered, local_weight, (((1,), (1,)), ((), ())), preferred_element_type=jnp.float32
         )

time: 681 us -> 828 us (1.22)
  waiting for transfers between devices: 360 us -> 448 us
  local copies, waits for them, and re-layouts: 10.6 us -> 51.9 us
    ppermute x0 -> x28, waiting for transfers between devices: none -> 391 us  [layer_block(): lax.ppermute(ring[-1], 'tensor', [(dev, (dev + 1) % 8) for dev in range(8)])]
    all_gather x4 -> x0, waiting for transfers between devices: 278 us -> none  [layer_block(): gathered = lax.all_gather(dy_rows, 'tensor', axis=1, tiled=True)]
    while x0 -> x124, local copies, waits for them, and re-layouts: none -> 38.7 us
    ppermute x4, waiting for transfers between devices: 24.1 us -> 0.1 us  [shifted(): return lax.ppermute(block, axis, route)]
  transfers between devices with their start and end apart: 10 -> 34, of which waited for: 10 -> 31; matrix products, arithmetic and copies ran while one was open for 11% -> 10% of each run, Pallas kernels for 0% -> 0%
where the time goes in v1:
time: 828 us; the launch traced here: 826 us
  waiting for transfers between devices  448 us (54%)
  matrix products  160 us (19%)
  blocking collectives  84.8 us (10%)
  other arithmetic  57.9 us (7%)
  local copies, waits for them, and re-layouts  51.9 us (6%)
  between operations  17.4 us (2%)
    ppermute x28, waiting for transfers between devices, layer_block(): lax.ppermute(ring[-1], 'tensor', [(dev, (dev + 1) % 8) for dev in range(8)])  391 us
    dot_general x4, matrix products, layer_block(): lax.dot_general(saved_rows, gathered, (((0,), (0,)), ((), ())), preferred...  64.4 us
    dot_general x4, matrix products, layer_block(): lax.dot_general(gathered, local_weight, (((1,), (1,)), ((), ())), preferr...  52.8 us
    while x124, local copies, waits for them, and re-layouts  38.7 us
    psum x2, blocking collectives, body(): lax.psum((jnp.sum(exponent, axis=1), jnp.sum(jnp.where(label_hit, logits,...  29.4 us
    all_gather x1, waiting for transfers between devices, body(): lax.all_gather(hidden_rows, 'tensor', axis=1, tiled=True)  29.1 us
    unnamed x3, waiting for transfers between devices  27.5 us
    psum x1, blocking collectives, body(): lax.psum((col_part, jnp.sum(row_new), jnp.sum(weight_float * weight_float...  26 us
  transfers between devices with their start and end apart: 34, of which 31 were waited for; matrix products, arithmetic and copies ran while one was open for 10% of the time, Pallas kernels for 0%

profile of v1, /device:TPU:0, one launch (start us, length us, event | category | flops | bytes accessed | tf_op | source)
XLA Modules:
  0.0 826.3 jit_solution(12617137264919196985)
XLA Ops:
  9.9 29.1 %all-gather.2.cloned.1.call-done = bf16[128,6656]{0,1:T(8,128)(2,1)} async-done(((bf16[128,832]{0,1:T(8,128)(2,1)}), bf16[128,6656]{0,1:T(8,128)(2,1)}) %all-gather.2.cloned.1.call-update) | async-done | bytes 1703952 | tf_op jit(solution)/shard_map/all_gather | solution.py:32
  39.0 22.1 %exponential_reduce_fusion = (f32[128]{0:T(128)S(1)}, f32[128]{0:T(128)}, f32[128,4000]{0,1:T(8,128)S(1)}) fusion(s32[4000]{0:T(1024)S(1)} %iota_add_fusion, s32[128]{0:T(128)S(1)} %dynamic_slice.18, bf16[6656,4000]{0,1:T(8,128)(2,1)} %param.11, bf16[128,6656]{0,1:T(8,128)(2,1)} %all-gather.2.cloned.1.call-done), kind=kOutput, calls=%fused_computation.42 | convolution fusion | flops 6817792000 | bytes 57017472 | tf_op jit(solution)/shard_map/dot_general | solution.py:31
  61.0 15.1 %psum.49 = f32[128]{0:T(128)S(1)} all-reduce(f32[128]{0:T(128)S(1)} %get-tuple-element.282), channel_id=1, replica_groups=mesh['section'=4,'tensor'=8] {'tensor'}, use_global_device_ids=true, to_apply=%region_1.2 | all-reduce | flops 128 | bytes 1024 | tf_op jit(solution)/shard_map/psum | solution.py:40
  76.2 20.9 %convolution_bitcast_fusion = f32[6656,128]{0,1:T(8,128)} fusion(bf16[6656,4000]{0,1:T(8,128)(2,1)} %param.11, f32[128,4000]{0,1:T(8,128)S(1)} %get-tuple-element.312, f32[128]{0:T(128)S(1)} %psum.49, s32[128]{0:T(128)S(1)} %dynamic_slice.18, s32[4000]{0:T(1024)S(1)} %iota_add_fusion), kind=kOutput, calls=%fused_computation.35 | convolution fusion | flops 6818816000 | bytes 58720896 | tf_op jit(solution)/shard_map/dot_general | solution.py:53
  115.5 27.4 %reduce-scatter.4.cloned.1.call-done = f32[832,128]{1,0:T(8,128)} async-done(((f32[6656,128]{1,0:T(8,128)}), f32[832,128]{1,0:T(8,128)}) %reduce-scatter.4.cloned.1.call-update) | async-done | bytes 426000
  144.1 12.6 %all_gather.7 = bf16[512,832]{1,0:T(8,128)(2,1)S(1)} all-gather(bf16[128,832]{1,0:T(8,128)(2,1)S(1)} %bitcast.29), channel_id=1, replica_groups=mesh['section'=4,'tensor'=8] {'section'}, dimensions={0}, use_global_device_ids=true | all-gather | bytes 1064960 | tf_op jit(solution)/shard_map/all_gather | solution.py:62
  159.0 558.7 %while.20 = (s32[]{:T(128)}, bf16[512,832]{0,1:T(8,128)(2,1)}, f32[832,6656]{1,0:T(8,128)}, bf16[512,832]{0,1:T(8,128)(2,1)}, pred[]{:T(512)}, /*index=5*/bf16[5...) while((s32[]{:T(128)}, bf16[512,832]{0,1:T(8,128)(2,1)}, ...), condition=%wide.region_8.9_spmd.clone, body=%wide.region_7.8_spmd.clone.sunk | while | flops 11360567296 | bytes 208733072 | solution.py:104
  160.3 13.9 %collective-permute-done = bf16[512,832]{0,1:T(8,128)(2,1)S(1)} collective-permute-done((bf16[512,832]{0,1:T(8,128)(2,1)S(1)}, bf16[512,832]{0,1:T(8,128)(2,1)S(1)}, u32[]{:S(2)}, u32[]{:S(2)}) %collective-permute-start) | collective-permute-done | bytes 852000 | tf_op jit(solution)/shard_map/while/body/eval_jaxpr/ppermute | solution.py:70
  174.2 13.9 %collective-permute-done.1 = bf16[512,832]{0,1:T(8,128)(2,1)S(1)} collective-permute-done((bf16[512,832]{0,1:T(8,128)(2,1)S(1)}, bf16[512,832]{0,1:T(8,128)(2,1)S(1)}, u32[]{:S(2)}, u32[]{:S(2)}) %collective-permute-start.1) | collective-permute-done | bytes 852000 | tf_op jit(solution)/shard_map/while/body/eval_jaxpr/ppermute | solution.py:70
  188.1 13.9 %collective-permute-done.2 = bf16[512,832]{0,1:T(8,128)(2,1)S(1)} collective-permute-done((bf16[512,832]{0,1:T(8,128)(2,1)S(1)}, bf16[512,832]{0,1:T(8,128)(2,1)S(1)}, u32[]{:S(2)}, u32[]{:S(2)}) %collective-permute-start.2) | collective-permute-done | bytes 852000 | tf_op jit(solution)/shard_map/while/body/eval_jaxpr/ppermute | solution.py:70
  202.1 13.9 %collective-permute-done.3 = bf16[512,832]{0,1:T(8,128)(2,1)S(1)} collective-permute-done((bf16[512,832]{0,1:T(8,128)(2,1)S(1)}, bf16[512,832]{0,1:T(8,128)(2,1)S(1)}, u32[]{:S(2)}, u32[]{:S(2)}) %collective-permute-start.3) | collective-permute-done | bytes 852000 | tf_op jit(solution)/shard_map/while/body/eval_jaxpr/ppermute | solution.py:70
  216.9 13.9 %collective-permute-done.4 = bf16[512,832]{0,1:T(8,128)(2,1)S(1)} collective-permute-done((bf16[512,832]{0,1:T(8,128)(2,1)S(1)}, bf16[512,832]{0,1:T(8,128)(2,1)S(1)}, u32[]{:S(2)}, u32[]{:S(2)}) %collective-permute-start.4) | collective-permute-done | bytes 852000 | tf_op jit(solution)/shard_map/while/body/eval_jaxpr/ppermute | solution.py:70
  231.7 14.0 %collective-permute-done.5 = bf16[512,832]{0,1:T(8,128)(2,1)} collective-permute-done((bf16[512,832]{0,1:T(8,128)(2,1)S(1)}, bf16[512,832]{0,1:T(8,128)(2,1)}, u32[]{:S(2)}, u32[]{:S(2)}) %collective-permute-start.5) | collective-permute-done | bytes 852000 | tf_op jit(solution)/shard_map/while/body/eval_jaxpr/ppermute | solution.py:70
  245.8 14.2 %collective-permute-done.6 = bf16[512,832]{0,1:T(8,128)(2,1)} collective-permute-done((bf16[512,832]{0,1:T(8,128)(2,1)}, bf16[512,832]{0,1:T(8,128)(2,1)}, u32[]{:S(2)}, u32[]{:S(2)}) %collective-permute-start.6) | collective-permute-done | bytes 852000 | tf_op jit(solution)/shard_map/while/body/eval_jaxpr/ppermute | solution.py:70
  268.0 13.2 %select_select_fusion.2 = (bf16[512,832]{0,1:T(8,128)(2,1)S(1)}, bf16[512,832]{0,1:T(8,128)(2,1)S(1)}) fusion(bf16[512,832]{0,1:T(8,128)(2,1)S(1)} %copy-done.16, pred[]{:T(512)S(6)} %compare.3, pred[]{:T(512)S(6)} %eq.62, bf16[832,6656]{1,0:T(8,128)(2,1)} %get-tuple-element.408, bf16[512,13312]{0,1:T(8,128)(2,1)S(1)} %constant_dynamic-update-slice_fusion.47, ...), kind=kOutput, calls=%fused_computation.5.clone.1 | convolution fusion | flops 5672828928 | bytes 21299206 | tf_op jit(solution)/shard_map/while/body/eval_jaxpr/dot_general | solution.py:77
  282.5 13.3 %bitcast_add_fusion.2 = f32[832,6656]{1,0:T(8,128)} fusion(f32[832,6656]{1,0:T(8,128)} %get-tuple-element.389, bf16[512,832]{1,0:T(8,128)(2,1)S(1)} %copy-done.7, pred[]{:T(512)S(6)} %compare.3, pred[]{:T(512)S(6)} %eq.62, bf16[512,13312]{0,1:T(8,128)(2,1)} %copy-done.2, s32[]{:T(128)S(6)} %select_n.143), kind=kOutput, calls=%fused_computation.clone.1 | convolution fusion | flops 5687312384 | bytes 51970056 | tf_op jit(solution)/shard_map/while/body/eval_jaxpr/dot_general | solution.py:80
  297.2 13.9 %collective-permute-done = bf16[512,832]{0,1:T(8,128)(2,1)S(1)} collective-permute-done((bf16[512,832]{0,1:T(8,128)(2,1)S(1)}, bf16[512,832]{0,1:T(8,128)(2,1)S(1)}, u32[]{:S(2)}, u32[]{:S(2)}) %collective-permute-start) | collective-permute-done | bytes 852000 | tf_op jit(solution)/shard_map/while/body/eval_jaxpr/ppermute | solution.py:70
  311.1 13.9 %collective-permute-done.1 = bf16[512,832]{0,1:T(8,128)(2,1)S(1)} collective-permute-done((bf16[512,832]{0,1:T(8,128)(2,1)S(1)}, bf16[512,832]{0,1:T(8,128)(2,1)S(1)}, u32[]{:S(2)}, u32[]{:S(2)}) %collective-permute-start.1) | collective-permute-done | bytes 852000 | tf_op jit(solution)/shard_map/while/body/eval_jaxpr/ppermute | solution.py:70
  325.0 13.9 %collective-permute-done.2 = bf16[512,832]{0,1:T(8,128)(2,1)S(1)} collective-permute-done((bf16[512,832]{0,1:T(8,128)(2,1)S(1)}, bf16[512,832]{0,1:T(8,128)(2,1)S(1)}, u32[]{:S(2)}, u32[]{:S(2)}) %collective-permute-start.2) | collective-permute-done | bytes 852000 | tf_op jit(solution)/shard_map/while/body/eval_jaxpr/ppermute | solution.py:70
  339.0 13.9 %collective-permute-done.3 = bf16[512,832]{0,1:T(8,128)(2,1)S(1)} collective-permute-done((bf16[512,832]{0,1:T(8,128)(2,1)S(1)}, bf16[512,832]{0,1:T(8,128)(2,1)S(1)}, u32[]{:S(2)}, u32[]{:S(2)}) %collective-permute-start.3) | collective-permute-done | bytes 852000 | tf_op jit(solution)/shard_map/while/body/eval_jaxpr/ppermute | solution.py:70
  353.8 13.9 %collective-permute-done.4 = bf16[512,832]{0,1:T(8,128)(2,1)S(1)} collective-permute-done((bf16[512,832]{0,1:T(8,128)(2,1)S(1)}, bf16[512,832]{0,1:T(8,128)(2,1)S(1)}, u32[]{:S(2)}, u32[]{:S(2)}) %collective-permute-start.4) | collective-permute-done | bytes 852000 | tf_op jit(solution)/shard_map/while/body/eval_jaxpr/ppermute | solution.py:70
  368.6 14.0 %collective-permute-done.5 = bf16[512,832]{0,1:T(8,128)(2,1)} collective-permute-done((bf16[512,832]{0,1:T(8,128)(2,1)S(1)}, bf16[512,832]{0,1:T(8,128)(2,1)}, u32[]{:S(2)}, u32[]{:S(2)}) %collective-permute-start.5) | collective-permute-done | bytes 852000 | tf_op jit(solution)/shard_map/while/body/eval_jaxpr/ppermute | solution.py:70
  382.7 14.2 %collective-permute-done.6 = bf16[512,832]{0,1:T(8,128)(2,1)} collective-permute-done((bf16[512,832]{0,1:T(8,128)(2,1)}, bf16[512,832]{0,1:T(8,128)(2,1)}, u32[]{:S(2)}, u32[]{:S(2)}) %collective-permute-start.6) | collective-permute-done | bytes 852000 | tf_op jit(solution)/shard_map/while/body/eval_jaxpr/ppermute | solution.py:70
  404.9 13.2 %select_select_fusion.2 = (bf16[512,832]{0,1:T(8,128)(2,1)S(1)}, bf16[512,832]{0,1:T(8,128)(2,1)S(1)}) fusion(bf16[512,832]{0,1:T(8,128)(2,1)S(1)} %copy-done.16, pred[]{:T(512)S(6)} %compare.3, pred[]{:T(512)S(6)} %eq.62, bf16[832,6656]{1,0:T(8,128)(2,1)} %get-tuple-element.408, bf16[512,13312]{0,1:T(8,128)(2,1)S(1)} %constant_dynamic-update-slice_fusion.47, ...), kind=kOutput, calls=%fused_computation.5.clone.1 | convolution fusion | flops 5672828928 | bytes 21299206 | tf_op jit(solution)/shard_map/while/body/eval_jaxpr/dot_general | solution.py:77
  419.5 17.0 %bitcast_add_fusion.2 = f32[832,6656]{1,0:T(8,128)} fusion(f32[832,6656]{1,0:T(8,128)} %get-tuple-element.389, bf16[512,832]{1,0:T(8,128)(2,1)S(1)} %copy-done.7, pred[]{:T(512)S(6)} %compare.3, pred[]{:T(512)S(6)} %eq.62, bf16[512,13312]{0,1:T(8,128)(2,1)} %copy-done.2, s32[]{:T(128)S(6)} %select_n.143), kind=kOutput, calls=%fused_computation.clone.1 | convolution fusion | flops 5687312384 | bytes 51970056 | tf_op jit(solution)/shard_map/while/body/eval_jaxpr/dot_general | solution.py:80
  437.8 13.9 %collective-permute-done = bf16[512,832]{0,1:T(8,128)(2,1)S(1)} collective-permute-done((bf16[512,832]{0,1:T(8,128)(2,1)S(1)}, bf16[512,832]{0,1:T(8,128)(2,1)S(1)}, u32[]{:S(2)}, u32[]{:S(2)}) %collective-permute-start) | collective-permute-done | bytes 852000 | tf_op jit(solution)/shard_map/while/body/eval_jaxpr/ppermute | solution.py:70
  451.7 13.9 %collective-permute-done.1 = bf16[512,832]{0,1:T(8,128)(2,1)S(1)} collective-permute-done((bf16[512,832]{0,1:T(8,128)(2,1)S(1)}, bf16[512,832]{0,1:T(8,128)(2,1)S(1)}, u32[]{:S(2)}, u32[]{:S(2)}) %collective-permute-start.1) | collective-permute-done | bytes 852000 | tf_op jit(solution)/shard_map/while/body/eval_jaxpr/ppermute | solution.py:70
  465.6 13.9 %collective-permute-done.2 = bf16[512,832]{0,1:T(8,128)(2,1)S(1)} collective-permute-done((bf16[512,832]{0,1:T(8,128)(2,1)S(1)}, bf16[512,832]{0,1:T(8,128)(2,1)S(1)}, u32[]{:S(2)}, u32[]{:S(2)}) %collective-permute-start.2) | collective-permute-done | bytes 852000 | tf_op jit(solution)/shard_map/while/body/eval_jaxpr/ppermute | solution.py:70
  479.6 13.9 %collective-permute-done.3 = bf16[512,832]{0,1:T(8,128)(2,1)S(1)} collective-permute-done((bf16[512,832]{0,1:T(8,128)(2,1)S(1)}, bf16[512,832]{0,1:T(8,128)(2,1)S(1)}, u32[]{:S(2)}, u32[]{:S(2)}) %collective-permute-start.3) | collective-permute-done | bytes 852000 | tf_op jit(solution)/shard_map/while/body/eval_jaxpr/ppermute | solution.py:70
  494.4 13.9 %collective-permute-done.4 = bf16[512,832]{0,1:T(8,128)(2,1)S(1)} collective-permute-done((bf16[512,832]{0,1:T(8,128)(2,1)S(1)}, bf16[512,832]{0,1:T(8,128)(2,1)S(1)}, u32[]{:S(2)}, u32[]{:S(2)}) %collective-permute-start.4) | collective-permute-done | bytes 852000 | tf_op jit(solution)/shard_map/while/body/eval_jaxpr/ppermute | solution.py:70
  509.2 14.0 %collective-permute-done.5 = bf16[512,832]{0,1:T(8,128)(2,1)} collective-permute-done((bf16[512,832]{0,1:T(8,128)(2,1)S(1)}, bf16[512,832]{0,1:T(8,128)(2,1)}, u32[]{:S(2)}, u32[]{:S(2)}) %collective-permute-start.5) | collective-permute-done | bytes 852000 | tf_op jit(solution)/shard_map/while/body/eval_jaxpr/ppermute | solution.py:70
  523.3 14.2 %collective-permute-done.6 = bf16[512,832]{0,1:T(8,128)(2,1)} collective-permute-done((bf16[512,832]{0,1:T(8,128)(2,1)}, bf16[512,832]{0,1:T(8,128)(2,1)}, u32[]{:S(2)}, u32[]{:S(2)}) %collective-permute-start.6) | collective-permute-done | bytes 852000 | tf_op jit(solution)/shard_map/while/body/eval_jaxpr/ppermute | solution.py:70
  545.5 13.2 %select_select_fusion.2 = (bf16[512,832]{0,1:T(8,128)(2,1)S(1)}, bf16[512,832]{0,1:T(8,128)(2,1)S(1)}) fusion(bf16[512,832]{0,1:T(8,128)(2,1)S(1)} %copy-done.16, pred[]{:T(512)S(6)} %compare.3, pred[]{:T(512)S(6)} %eq.62, bf16[832,6656]{1,0:T(8,128)(2,1)} %get-tuple-element.408, bf16[512,13312]{0,1:T(8,128)(2,1)S(1)} %constant_dynamic-update-slice_fusion.47, ...), kind=kOutput, calls=%fused_computation.5.clone.1 | convolution fusion | flops 5672828928 | bytes 21299206 | tf_op jit(solution)/shard_map/while/body/eval_jaxpr/dot_general | solution.py:77
  560.0 17.0 %bitcast_add_fusion.2 = f32[832,6656]{1,0:T(8,128)} fusion(f32[832,6656]{1,0:T(8,128)} %get-tuple-element.389, bf16[512,832]{1,0:T(8,128)(2,1)S(1)} %copy-done.7, pred[]{:T(512)S(6)} %compare.3, pred[]{:T(512)S(6)} %eq.62, bf16[512,13312]{0,1:T(8,128)(2,1)} %copy-done.2, s32[]{:T(128)S(6)} %select_n.143), kind=kOutput, calls=%fused_computation.clone.1 | convolution fusion | flops 5687312384 | bytes 51970056 | tf_op jit(solution)/shard_map/while/body/eval_jaxpr/dot_general | solution.py:80
  578.4 13.9 %collective-permute-done = bf16[512,832]{0,1:T(8,128)(2,1)S(1)} collective-permute-done((bf16[512,832]{0,1:T(8,128)(2,1)S(1)}, bf16[512,832]{0,1:T(8,128)(2,1)S(1)}, u32[]{:S(2)}, u32[]{:S(2)}) %collective-permute-start) | collective-permute-done | bytes 852000 | tf_op jit(solution)/shard_map/while/body/eval_jaxpr/ppermute | solution.py:70
  592.3 13.9 %collective-permute-done.1 = bf16[512,832]{0,1:T(8,128)(2,1)S(1)} collective-permute-done((bf16[512,832]{0,1:T(8,128)(2,1)S(1)}, bf16[512,832]{0,1:T(8,128)(2,1)S(1)}, u32[]{:S(2)}, u32[]{:S(2)}) %collective-permute-start.1) | collective-permute-done | bytes 852000 | tf_op jit(solution)/shard_map/while/body/eval_jaxpr/ppermute | solution.py:70
  606.2 13.9 %collective-permute-done.2 = bf16[512,832]{0,1:T(8,128)(2,1)S(1)} collective-permute-done((bf16[512,832]{0,1:T(8,128)(2,1)S(1)}, bf16[512,832]{0,1:T(8,128)(2,1)S(1)}, u32[]{:S(2)}, u32[]{:S(2)}) %collective-permute-start.2) | collective-permute-done | bytes 852000 | tf_op jit(solution)/shard_map/while/body/eval_jaxpr/ppermute | solution.py:70
  620.2 13.9 %collective-permute-done.3 = bf16[512,832]{0,1:T(8,128)(2,1)S(1)} collective-permute-done((bf16[512,832]{0,1:T(8,128)(2,1)S(1)}, bf16[512,832]{0,1:T(8,128)(2,1)S(1)}, u32[]{:S(2)}, u32[]{:S(2)}) %collective-permute-start.3) | collective-permute-done | bytes 852000 | tf_op jit(solution)/shard_map/while/body/eval_jaxpr/ppermute | solution.py:70
  635.0 13.9 %collective-permute-done.4 = bf16[512,832]{0,1:T(8,128)(2,1)S(1)} collective-permute-done((bf16[512,832]{0,1:T(8,128)(2,1)S(1)}, bf16[512,832]{0,1:T(8,128)(2,1)S(1)}, u32[]{:S(2)}, u32[]{:S(2)}) %collective-permute-start.4) | collective-permute-done | bytes 852000 | tf_op jit(solution)/shard_map/while/body/eval_jaxpr/ppermute | solution.py:70
  649.8 14.0 %collective-permute-done.5 = bf16[512,832]{0,1:T(8,128)(2,1)} collective-permute-done((bf16[512,832]{0,1:T(8,128)(2,1)S(1)}, bf16[512,832]{0,1:T(8,128)(2,1)}, u32[]{:S(2)}, u32[]{:S(2)}) %collective-permute-start.5) | collective-permute-done | bytes 852000 | tf_op jit(solution)/shard_map/while/body/eval_jaxpr/ppermute | solution.py:70
  663.9 14.2 %collective-permute-done.6 = bf16[512,832]{0,1:T(8,128)(2,1)} collective-permute-done((bf16[512,832]{0,1:T(8,128)(2,1)}, bf16[512,832]{0,1:T(8,128)(2,1)}, u32[]{:S(2)}, u32[]{:S(2)}) %collective-permute-start.6) | collective-permute-done | bytes 852000 | tf_op jit(solution)/shard_map/while/body/eval_jaxpr/ppermute | solution.py:70
  686.1 13.2 %select_select_fusion.2 = (bf16[512,832]{0,1:T(8,128)(2,1)S(1)}, bf16[512,832]{0,1:T(8,128)(2,1)S(1)}) fusion(bf16[512,832]{0,1:T(8,128)(2,1)S(1)} %copy-done.16, pred[]{:T(512)S(6)} %compare.3, pred[]{:T(512)S(6)} %eq.62, bf16[832,6656]{1,0:T(8,128)(2,1)} %get-tuple-element.408, bf16[512,13312]{0,1:T(8,128)(2,1)S(1)} %constant_dynamic-update-slice_fusion.47, ...), kind=kOutput, calls=%fused_computation.5.clone.1 | convolution fusion | flops 5672828928 | bytes 21299206 | tf_op jit(solution)/shard_map/while/body/eval_jaxpr/dot_general | solution.py:77
  700.6 17.0 %bitcast_add_fusion.2 = f32[832,6656]{1,0:T(8,128)} fusion(f32[832,6656]{1,0:T(8,128)} %get-tuple-element.389, bf16[512,832]{1,0:T(8,128)(2,1)S(1)} %copy-done.7, pred[]{:T(512)S(6)} %compare.3, pred[]{:T(512)S(6)} %eq.62, bf16[512,13312]{0,1:T(8,128)(2,1)} %copy-done.2, s32[]{:T(128)S(6)} %select_n.143), kind=kOutput, calls=%fused_computation.clone.1 | convolution fusion | flops 5687312384 | bytes 51970056 | tf_op jit(solution)/shard_map/while/body/eval_jaxpr/dot_general | solution.py:80
  728.0 26.0 %all-reduce.1 = (f32[]{:T(128)}, f32[6656]{0:T(1024)S(1)}) all-reduce(f32[]{:T(128)} %get-tuple-element.307, f32[6656]{0:T(1024)S(1)} %get-tuple-element.280), channel_id=1, replica_groups=mesh['section'=4,'tensor'=8] {'tensor'}, use_global_device_ids=true, to_apply=%region_15.16 | all-reduce | flops 6657 | bytes 53256 | tf_op jit(solution)/shard_map/psum | solution.py:112
  754.1 11.9 %multiply_reduce_fusion = f32[]{:T(128)} fusion(f32[832,6656]{1,0:T(8,128)} %get-tuple-element.231, f32[]{:T(128)} %get-tuple-element.305, f32[6656]{0:T(1024)S(1)} %multiply_add_fusion.1, f32[832]{0:T(1024)S(1)} %get-tuple-element.308), kind=kLoop, calls=%fused_computation.29 | loop fusion | flops 27688960 | bytes 22181128 | tf_op jit(solution)/shard_map/reduce_sum | solution.py:117
  766.0 14.2 %all-reduce = (f32[128]{0:T(128)S(1)}, f32[]{:T(128)}, f32[]{:T(128)}) all-reduce(f32[128]{0:T(128)S(1)} %copy-done.18, f32[]{:T(128)} %fusion.7, f32[]{:T(128)} %multiply_reduce_fusion), channel_id=1, replica_groups=mesh['section'=4,'tensor'=8] {'tensor'}, use_global_device_ids=true, to_apply=%region_3.4 | all-reduce | flops 130 | bytes 1040 | tf_op jit(solution)/shard_map/psum | solution.py:40
  781.7 17.4 %fusion.11 = bf16[1,832,6656]{2,1,0:T(8,128)(2,1)} fusion(f32[]{:T(128)S(6)} %div.49, bf16[1,832,6656]{2,1,0:T(8,128)(2,1)} %bitcast.27, f32[832,6656]{1,0:T(8,128)} %get-tuple-element.231, f32[]{:T(128)} %get-tuple-element.305, f32[6656]{0:T(1024)S(1)} %multiply_add_fusion.1, f32[832]{0:T(1024)S(1)} %get-tuple-element.308), kind=kLoop, calls=%fused_computation.34 | loop fusion | flops 38764544 | bytes 44332296 | tf_op jit(solution)/shard_map/broadcast_in_dim | solution.py:124
  800.3 16.8 %psum.51 = f32[]{:T(128)} all-reduce(f32[]{:T(128)} %subtract_reduce_fusion), channel_id=1, replica_groups=mesh['section'=4,'tensor'=8] {'section'}, use_global_device_ids=true, to_apply=%region_5.6 | all-reduce | flops 1 | bytes 8 | tf_op jit(solution)/shard_map/psum | solution.py:63
  (213 shorter events, 86.1 us)
Async XLA Ops:
  7.2 31.8 %all-gather.2.cloned.1.call-start = ((), (), s32[]{:S(2)}) async-start(), calls=%async_computation.1 | async-start | bytes 1916928 | tf_op jit(solution)/shard_map/all_gather | solution.py:32
  9.1 133.9 %reduce-scatter.4.cloned.1.call-start = ((), (), s32[]{:S(2)}) async-start(), calls=%async_computation.2 | async-start | bytes 3833856
  76.2 26.0 %copy-start.8 = (bf16[1,512,832]{1,2,0:T(8,128)(2,1)S(1)}, bf16[1,512,832]{1,2,0:T(8,128)(2,1)}, u32[]{:S(2)}) copy-start(bf16[1,512,832]{1,2,0:T(8,128)(2,1)} %param.12) | copy-start | bytes 2555908
  76.2 27.3 %copy-start.12 = (f32[1,832]{1,0:T(1,128)S(1)}, f32[1,832]{1,0:T(1,128)}, u32[]{:S(2)}) copy-start(f32[1,832]{1,0:T(1,128)} %param.14) | copy-start | bytes 9988
  76.2 27.9 %copy-start.10 = (f32[1,6656]{1,0:T(1,128)S(1)}, f32[1,6656]{1,0:T(1,128)}, u32[]{:S(2)}) copy-start(f32[1,6656]{1,0:T(1,128)} %param.15) | copy-start | bytes 79876
  160.3 14.0 %collective-permute-start = (bf16[512,832]{0,1:T(8,128)(2,1)S(1)}, bf16[512,832]{0,1:T(8,128)(2,1)S(1)}, u32[]{:S(2)}, u32[]{:S(2)}) collective-permute-start(bf16[512,832]{0,1:T(8,128)(2,1)S(1)} %broadcast_select_fusion.2), channel_id=1, source_target_pairs={{0,1},{1,2},{2,3},{3,4},{4,5},{5,6},{6,7},{7,0},{8,9},{9,10},{10,1... | collective-permute-start | bytes 2555912 | tf_op jit(solution)/shard_map/while/body/eval_jaxpr/ppermute | solution.py:70
  174.2 13.9 %collective-permute-start.1 = (bf16[512,832]{0,1:T(8,128)(2,1)S(1)}, bf16[512,832]{0,1:T(8,128)(2,1)S(1)}, u32[]{:S(2)}, u32[]{:S(2)}) collective-permute-start(bf16[512,832]{0,1:T(8,128)(2,1)S(1)} %collective-permute-done), channel_id=1, source_target_pairs={{0,1},{1,2},{2,3},{3,4},{4,5},{5,6},{6,7},{7,0},{8,9},{9,10},{10,1... | collective-permute-start | bytes 2555912 | tf_op jit(solution)/shard_map/while/body/eval_jaxpr/ppermute | solution.py:70
  188.1 13.9 %collective-permute-start.2 = (bf16[512,832]{0,1:T(8,128)(2,1)S(1)}, bf16[512,832]{0,1:T(8,128)(2,1)S(1)}, u32[]{:S(2)}, u32[]{:S(2)}) collective-permute-start(bf16[512,832]{0,1:T(8,128)(2,1)S(1)} %collective-permute-done.1), channel_id=1, source_target_pairs={{0,1},{1,2},{2,3},{3,4},{4,5},{5,6},{6,7},{7,0},{8,9},{9,10},{10,1... | collective-permute-start | bytes 2555912 | tf_op jit(solution)/shard_map/while/body/eval_jaxpr/ppermute | solution.py:70
  202.1 13.9 %collective-permute-start.3 = (bf16[512,832]{0,1:T(8,128)(2,1)S(1)}, bf16[512,832]{0,1:T(8,128)(2,1)S(1)}, u32[]{:S(2)}, u32[]{:S(2)}) collective-permute-start(bf16[512,832]{0,1:T(8,128)(2,1)S(1)} %collective-permute-done.2), channel_id=1, source_target_pairs={{0,1},{1,2},{2,3},{3,4},{4,5},{5,6},{6,7},{7,0},{8,9},{9,10},{10,1... | collective-permute-start | bytes 2555912 | tf_op jit(solution)/shard_map/while/body/eval_jaxpr/ppermute | solution.py:70
  216.9 13.9 %collective-permute-start.4 = (bf16[512,832]{0,1:T(8,128)(2,1)S(1)}, bf16[512,832]{0,1:T(8,128)(2,1)S(1)}, u32[]{:S(2)}, u32[]{:S(2)}) collective-permute-start(bf16[512,832]{0,1:T(8,128)(2,1)S(1)} %collective-permute-done.3), channel_id=1, source_target_pairs={{0,1},{1,2},{2,3},{3,4},{4,5},{5,6},{6,7},{7,0},{8,9},{9,10},{10,1... | collective-permute-start | bytes 2555912 | tf_op jit(solution)/shard_map/while/body/eval_jaxpr/ppermute | solution.py:70
  231.7 14.0 %collective-permute-start.5 = (bf16[512,832]{0,1:T(8,128)(2,1)S(1)}, bf16[512,832]{0,1:T(8,128)(2,1)}, u32[]{:S(2)}, u32[]{:S(2)}) collective-permute-start(bf16[512,832]{0,1:T(8,128)(2,1)S(1)} %collective-permute-done.4), channel_id=1, source_target_pairs={{0,1},{1,2},{2,3},{3,4},{4,5},{5,6},{6,7},{7,0},{8,9},{9,10},{10,1... | collective-permute-start | bytes 2555912 | tf_op jit(solution)/shard_map/while/body/eval_jaxpr/ppermute | solution.py:70
  245.8 14.2 %collective-permute-start.6 = (bf16[512,832]{0,1:T(8,128)(2,1)}, bf16[512,832]{0,1:T(8,128)(2,1)}, u32[]{:S(2)}, u32[]{:S(2)}) collective-permute-start(bf16[512,832]{0,1:T(8,128)(2,1)} %collective-permute-done.5), channel_id=1, source_target_pairs={{0,1},{1,2},{2,3},{3,4},{4,5},{5,6},{6,7},{7,0},{8,9},{9,10},{10,1... | collective-permute-start | bytes 2555912 | tf_op jit(solution)/shard_map/while/body/eval_jaxpr/ppermute | solution.py:70
  245.8 21.9 %copy-start.4 = (bf16[512,832]{0,1:T(8,128)(2,1)S(1)}, bf16[512,832]{0,1:T(8,128)(2,1)}, u32[]{:S(2)}) copy-start(bf16[512,832]{0,1:T(8,128)(2,1)} %copy-done.3) | copy-start | bytes 2555908 | tf_op jit(solution)/shard_map/while
  245.8 22.2 %copy-start.16 = (bf16[512,832]{0,1:T(8,128)(2,1)S(1)}, bf16[512,832]{0,1:T(8,128)(2,1)}, u32[]{:S(2)}) copy-start(bf16[512,832]{0,1:T(8,128)(2,1)} %get-tuple-element.390) | copy-start | bytes 2555908 | tf_op jit(solution)/shard_map/while
  281.2 14.7 %collective-permute-start.7 = (bf16[512,832]{0,1:T(8,128)(2,1)S(1)}, bf16[512,832]{0,1:T(8,128)(2,1)}, u32[]{:S(2)}, u32[]{:S(2)}) collective-permute-start(bf16[512,832]{0,1:T(8,128)(2,1)S(1)} %get-tuple-element.370), channel_id=1, source_target_pairs={{8,0},{16,8},{24,16},{9,1},{17,9},{25,17},{10,2},{18,10},{26,18},{... | collective-permute-start | bytes 2555912 | tf_op jit(solution)/shard_map/while/body/eval_jaxpr/ppermute | solution.py:14
  297.2 14.0 %collective-permute-start = (bf16[512,832]{0,1:T(8,128)(2,1)S(1)}, bf16[512,832]{0,1:T(8,128)(2,1)S(1)}, u32[]{:S(2)}, u32[]{:S(2)}) collective-permute-start(bf16[512,832]{0,1:T(8,128)(2,1)S(1)} %broadcast_select_fusion.2), channel_id=1, source_target_pairs={{0,1},{1,2},{2,3},{3,4},{4,5},{5,6},{6,7},{7,0},{8,9},{9,10},{10,1... | collective-permute-start | bytes 2555912 | tf_op jit(solution)/shard_map/while/body/eval_jaxpr/ppermute | solution.py:70
  311.1 13.9 %collective-permute-start.1 = (bf16[512,832]{0,1:T(8,128)(2,1)S(1)}, bf16[512,832]{0,1:T(8,128)(2,1)S(1)}, u32[]{:S(2)}, u32[]{:S(2)}) collective-permute-start(bf16[512,832]{0,1:T(8,128)(2,1)S(1)} %collective-permute-done), channel_id=1, source_target_pairs={{0,1},{1,2},{2,3},{3,4},{4,5},{5,6},{6,7},{7,0},{8,9},{9,10},{10,1... | collective-permute-start | bytes 2555912 | tf_op jit(solution)/shard_map/while/body/eval_jaxpr/ppermute | solution.py:70
  325.0 13.9 %collective-permute-start.2 = (bf16[512,832]{0,1:T(8,128)(2,1)S(1)}, bf16[512,832]{0,1:T(8,128)(2,1)S(1)}, u32[]{:S(2)}, u32[]{:S(2)}) collective-permute-start(bf16[512,832]{0,1:T(8,128)(2,1)S(1)} %collective-permute-done.1), channel_id=1, source_target_pairs={{0,1},{1,2},{2,3},{3,4},{4,5},{5,6},{6,7},{7,0},{8,9},{9,10},{10,1... | collective-permute-start | bytes 2555912 | tf_op jit(solution)/shard_map/while/body/eval_jaxpr/ppermute | solution.py:70
  339.0 13.9 %collective-permute-start.3 = (bf16[512,832]{0,1:T(8,128)(2,1)S(1)}, bf16[512,832]{0,1:T(8,128)(2,1)S(1)}, u32[]{:S(2)}, u32[]{:S(2)}) collective-permute-start(bf16[512,832]{0,1:T(8,128)(2,1)S(1)} %collective-permute-done.2), channel_id=1, source_target_pairs={{0,1},{1,2},{2,3},{3,4},{4,5},{5,6},{6,7},{7,0},{8,9},{9,10},{10,1... | collective-permute-start | bytes 2555912 | tf_op jit(solution)/shard_map/while/body/eval_jaxpr/ppermute | solution.py:70
  353.8 13.9 %collective-permute-start.4 = (bf16[512,832]{0,1:T(8,128)(2,1)S(1)}, bf16[512,832]{0,1:T(8,128)(2,1)S(1)}, u32[]{:S(2)}, u32[]{:S(2)}) collective-permute-start(bf16[512,832]{0,1:T(8,128)(2,1)S(1)} %collective-permute-done.3), channel_id=1, source_target_pairs={{0,1},{1,2},{2,3},{3,4},{4,5},{5,6},{6,7},{7,0},{8,9},{9,10},{10,1... | collective-permute-start | bytes 2555912 | tf_op jit(solution)/shard_map/while/body/eval_jaxpr/ppermute | solution.py:70
  368.6 14.0 %collective-permute-start.5 = (bf16[512,832]{0,1:T(8,128)(2,1)S(1)}, bf16[512,832]{0,1:T(8,128)(2,1)}, u32[]{:S(2)}, u32[]{:S(2)}) collective-permute-start(bf16[512,832]{0,1:T(8,128)(2,1)S(1)} %collective-permute-done.4), channel_id=1, source_target_pairs={{0,1},{1,2},{2,3},{3,4},{4,5},{5,6},{6,7},{7,0},{8,9},{9,10},{10,1... | collective-permute-start | bytes 2555912 | tf_op jit(solution)/shard_map/while/body/eval_jaxpr/ppermute | solution.py:70
  382.7 14.2 %collective-permute-start.6 = (bf16[512,832]{0,1:T(8,128)(2,1)}, bf16[512,832]{0,1:T(8,128)(2,1)}, u32[]{:S(2)}, u32[]{:S(2)}) collective-permute-start(bf16[512,832]{0,1:T(8,128)(2,1)} %collective-permute-done.5), channel_id=1, source_target_pairs={{0,1},{1,2},{2,3},{3,4},{4,5},{5,6},{6,7},{7,0},{8,9},{9,10},{10,1... | collective-permute-start | bytes 2555912 | tf_op jit(solution)/shard_map/while/body/eval_jaxpr/ppermute | solution.py:70
  382.7 21.9 %copy-start.4 = (bf16[512,832]{0,1:T(8,128)(2,1)S(1)}, bf16[512,832]{0,1:T(8,128)(2,1)}, u32[]{:S(2)}) copy-start(bf16[512,832]{0,1:T(8,128)(2,1)} %copy-done.3) | copy-start | bytes 2555908 | tf_op jit(solution)/shard_map/while
  382.7 22.2 %copy-start.16 = (bf16[512,832]{0,1:T(8,128)(2,1)S(1)}, bf16[512,832]{0,1:T(8,128)(2,1)}, u32[]{:S(2)}) copy-start(bf16[512,832]{0,1:T(8,128)(2,1)} %get-tuple-element.390) | copy-start | bytes 2555908 | tf_op jit(solution)/shard_map/while
  418.1 18.4 %collective-permute-start.7 = (bf16[512,832]{0,1:T(8,128)(2,1)S(1)}, bf16[512,832]{0,1:T(8,128)(2,1)}, u32[]{:S(2)}, u32[]{:S(2)}) collective-permute-start(bf16[512,832]{0,1:T(8,128)(2,1)S(1)} %get-tuple-element.370), channel_id=1, source_target_pairs={{8,0},{16,8},{24,16},{9,1},{17,9},{25,17},{10,2},{18,10},{26,18},{... | collective-permute-start | bytes 2555912 | tf_op jit(solution)/shard_map/while/body/eval_jaxpr/ppermute | solution.py:14
  437.8 14.0 %collective-permute-start = (bf16[512,832]{0,1:T(8,128)(2,1)S(1)}, bf16[512,832]{0,1:T(8,128)(2,1)S(1)}, u32[]{:S(2)}, u32[]{:S(2)}) collective-permute-start(bf16[512,832]{0,1:T(8,128)(2,1)S(1)} %broadcast_select_fusion.2), channel_id=1, source_target_pairs={{0,1},{1,2},{2,3},{3,4},{4,5},{5,6},{6,7},{7,0},{8,9},{9,10},{10,1... | collective-permute-start | bytes 2555912 | tf_op jit(solution)/shard_map/while/body/eval_jaxpr/ppermute | solution.py:70
  451.7 13.9 %collective-permute-start.1 = (bf16[512,832]{0,1:T(8,128)(2,1)S(1)}, bf16[512,832]{0,1:T(8,128)(2,1)S(1)}, u32[]{:S(2)}, u32[]{:S(2)}) collective-permute-start(bf16[512,832]{0,1:T(8,128)(2,1)S(1)} %collective-permute-done), channel_id=1, source_target_pairs={{0,1},{1,2},{2,3},{3,4},{4,5},{5,6},{6,7},{7,0},{8,9},{9,10},{10,1... | collective-permute-start | bytes 2555912 | tf_op jit(solution)/shard_map/while/body/eval_jaxpr/ppermute | solution.py:70
  465.6 13.9 %collective-permute-start.2 = (bf16[512,832]{0,1:T(8,128)(2,1)S(1)}, bf16[512,832]{0,1:T(8,128)(2,1)S(1)}, u32[]{:S(2)}, u32[]{:S(2)}) collective-permute-start(bf16[512,832]{0,1:T(8,128)(2,1)S(1)} %collective-permute-done.1), channel_id=1, source_target_pairs={{0,1},{1,2},{2,3},{3,4},{4,5},{5,6},{6,7},{7,0},{8,9},{9,10},{10,1... | collective-permute-start | bytes 2555912 | tf_op jit(solution)/shard_map/while/body/eval_jaxpr/ppermute | solution.py:70
  479.6 13.9 %collective-permute-start.3 = (bf16[512,832]{0,1:T(8,128)(2,1)S(1)}, bf16[512,832]{0,1:T(8,128)(2,1)S(1)}, u32[]{:S(2)}, u32[]{:S(2)}) collective-permute-start(bf16[512,832]{0,1:T(8,128)(2,1)S(1)} %collective-permute-done.2), channel_id=1, source_target_pairs={{0,1},{1,2},{2,3},{3,4},{4,5},{5,6},{6,7},{7,0},{8,9},{9,10},{10,1... | collective-permute-start | bytes 2555912 | tf_op jit(solution)/shard_map/while/body/eval_jaxpr/ppermute | solution.py:70
  494.4 13.9 %collective-permute-start.4 = (bf16[512,832]{0,1:T(8,128)(2,1)S(1)}, bf16[512,832]{0,1:T(8,128)(2,1)S(1)}, u32[]{:S(2)}, u32[]{:S(2)}) collective-permute-start(bf16[512,832]{0,1:T(8,128)(2,1)S(1)} %collective-permute-done.3), channel_id=1, source_target_pairs={{0,1},{1,2},{2,3},{3,4},{4,5},{5,6},{6,7},{7,0},{8,9},{9,10},{10,1... | collective-permute-start | bytes 2555912 | tf_op jit(solution)/shard_map/while/body/eval_jaxpr/ppermute | solution.py:70
  509.2 14.0 %collective-permute-start.5 = (bf16[512,832]{0,1:T(8,128)(2,1)S(1)}, bf16[512,832]{0,1:T(8,128)(2,1)}, u32[]{:S(2)}, u32[]{:S(2)}) collective-permute-start(bf16[512,832]{0,1:T(8,128)(2,1)S(1)} %collective-permute-done.4), channel_id=1, source_target_pairs={{0,1},{1,2},{2,3},{3,4},{4,5},{5,6},{6,7},{7,0},{8,9},{9,10},{10,1... | collective-permute-start | bytes 2555912 | tf_op jit(solution)/shard_map/while/body/eval_jaxpr/ppermute | solution.py:70
  523.3 14.2 %collective-permute-start.6 = (bf16[512,832]{0,1:T(8,128)(2,1)}, bf16[512,832]{0,1:T(8,128)(2,1)}, u32[]{:S(2)}, u32[]{:S(2)}) collective-permute-start(bf16[512,832]{0,1:T(8,128)(2,1)} %collective-permute-done.5), channel_id=1, source_target_pairs={{0,1},{1,2},{2,3},{3,4},{4,5},{5,6},{6,7},{7,0},{8,9},{9,10},{10,1... | collective-permute-start | bytes 2555912 | tf_op jit(solution)/shard_map/while/body/eval_jaxpr/ppermute | solution.py:70
  523.3 21.9 %copy-start.4 = (bf16[512,832]{0,1:T(8,128)(2,1)S(1)}, bf16[512,832]{0,1:T(8,128)(2,1)}, u32[]{:S(2)}) copy-start(bf16[512,832]{0,1:T(8,128)(2,1)} %copy-done.3) | copy-start | bytes 2555908 | tf_op jit(solution)/shard_map/while
  523.3 22.2 %copy-start.16 = (bf16[512,832]{0,1:T(8,128)(2,1)S(1)}, bf16[512,832]{0,1:T(8,128)(2,1)}, u32[]{:S(2)}) copy-start(bf16[512,832]{0,1:T(8,128)(2,1)} %get-tuple-element.390) | copy-start | bytes 2555908 | tf_op jit(solution)/shard_map/while
  558.7 18.4 %collective-permute-start.7 = (bf16[512,832]{0,1:T(8,128)(2,1)S(1)}, bf16[512,832]{0,1:T(8,128)(2,1)}, u32[]{:S(2)}, u32[]{:S(2)}) collective-permute-start(bf16[512,832]{0,1:T(8,128)(2,1)S(1)} %get-tuple-element.370), channel_id=1, source_target_pairs={{8,0},{16,8},{24,16},{9,1},{17,9},{25,17},{10,2},{18,10},{26,18},{... | collective-permute-start | bytes 2555912 | tf_op jit(solution)/shard_map/while/body/eval_jaxpr/ppermute | solution.py:14
  578.3 14.0 %collective-permute-start = (bf16[512,832]{0,1:T(8,128)(2,1)S(1)}, bf16[512,832]{0,1:T(8,128)(2,1)S(1)}, u32[]{:S(2)}, u32[]{:S(2)}) collective-permute-start(bf16[512,832]{0,1:T(8,128)(2,1)S(1)} %broadcast_select_fusion.2), channel_id=1, source_target_pairs={{0,1},{1,2},{2,3},{3,4},{4,5},{5,6},{6,7},{7,0},{8,9},{9,10},{10,1... | collective-permute-start | bytes 2555912 | tf_op jit(solution)/shard_map/while/body/eval_jaxpr/ppermute | solution.py:70
  592.3 13.9 %collective-permute-start.1 = (bf16[512,832]{0,1:T(8,128)(2,1)S(1)}, bf16[512,832]{0,1:T(8,128)(2,1)S(1)}, u32[]{:S(2)}, u32[]{:S(2)}) collective-permute-start(bf16[512,832]{0,1:T(8,128)(2,1)S(1)} %collective-permute-done), channel_id=1, source_target_pairs={{0,1},{1,2},{2,3},{3,4},{4,5},{5,6},{6,7},{7,0},{8,9},{9,10},{10,1... | collective-permute-start | bytes 2555912 | tf_op jit(solution)/shard_map/while/body/eval_jaxpr/ppermute | solution.py:70
  606.2 13.9 %collective-permute-start.2 = (bf16[512,832]{0,1:T(8,128)(2,1)S(1)}, bf16[512,832]{0,1:T(8,128)(2,1)S(1)}, u32[]{:S(2)}, u32[]{:S(2)}) collective-permute-start(bf16[512,832]{0,1:T(8,128)(2,1)S(1)} %collective-permute-done.1), channel_id=1, source_target_pairs={{0,1},{1,2},{2,3},{3,4},{4,5},{5,6},{6,7},{7,0},{8,9},{9,10},{10,1... | collective-permute-start | bytes 2555912 | tf_op jit(solution)/shard_map/while/body/eval_jaxpr/ppermute | solution.py:70
  620.1 13.9 %collective-permute-start.3 = (bf16[512,832]{0,1:T(8,128)(2,1)S(1)}, bf16[512,832]{0,1:T(8,128)(2,1)S(1)}, u32[]{:S(2)}, u32[]{:S(2)}) collective-permute-start(bf16[512,832]{0,1:T(8,128)(2,1)S(1)} %collective-permute-done.2), channel_id=1, source_target_pairs={{0,1},{1,2},{2,3},{3,4},{4,5},{5,6},{6,7},{7,0},{8,9},{9,10},{10,1... | collective-permute-start | bytes 2555912 | tf_op jit(solution)/shard_map/while/body/eval_jaxpr/ppermute | solution.py:70
  635.0 13.9 %collective-permute-start.4 = (bf16[512,832]{0,1:T(8,128)(2,1)S(1)}, bf16[512,832]{0,1:T(8,128)(2,1)S(1)}, u32[]{:S(2)}, u32[]{:S(2)}) collective-permute-start(bf16[512,832]{0,1:T(8,128)(2,1)S(1)} %collective-permute-done.3), channel_id=1, source_target_pairs={{0,1},{1,2},{2,3},{3,4},{4,5},{5,6},{6,7},{7,0},{8,9},{9,10},{10,1... | collective-permute-start | bytes 2555912 | tf_op jit(solution)/shard_map/while/body/eval_jaxpr/ppermute | solution.py:70
  649.8 14.0 %collective-permute-start.5 = (bf16[512,832]{0,1:T(8,128)(2,1)S(1)}, bf16[512,832]{0,1:T(8,128)(2,1)}, u32[]{:S(2)}, u32[]{:S(2)}) collective-permute-start(bf16[512,832]{0,1:T(8,128)(2,1)S(1)} %collective-permute-done.4), channel_id=1, source_target_pairs={{0,1},{1,2},{2,3},{3,4},{4,5},{5,6},{6,7},{7,0},{8,9},{9,10},{10,1... | collective-permute-start | bytes 2555912 | tf_op jit(solution)/shard_map/while/body/eval_jaxpr/ppermute | solution.py:70
  663.8 14.2 %collective-permute-start.6 = (bf16[512,832]{0,1:T(8,128)(2,1)}, bf16[512,832]{0,1:T(8,128)(2,1)}, u32[]{:S(2)}, u32[]{:S(2)}) collective-permute-start(bf16[512,832]{0,1:T(8,128)(2,1)} %collective-permute-done.5), channel_id=1, source_target_pairs={{0,1},{1,2},{2,3},{3,4},{4,5},{5,6},{6,7},{7,0},{8,9},{9,10},{10,1... | collective-permute-start | bytes 2555912 | tf_op jit(solution)/shard_map/while/body/eval_jaxpr/ppermute | solution.py:70
  663.9 22.2 %copy-start.16 = (bf16[512,832]{0,1:T(8,128)(2,1)S(1)}, bf16[512,832]{0,1:T(8,128)(2,1)}, u32[]{:S(2)}) copy-start(bf16[512,832]{0,1:T(8,128)(2,1)} %get-tuple-element.390) | copy-start | bytes 2555908 | tf_op jit(solution)/shard_map/while
  699.3 18.4 %collective-permute-start.7 = (bf16[512,832]{0,1:T(8,128)(2,1)S(1)}, bf16[512,832]{0,1:T(8,128)(2,1)}, u32[]{:S(2)}, u32[]{:S(2)}) collective-permute-start(bf16[512,832]{0,1:T(8,128)(2,1)S(1)} %get-tuple-element.370), channel_id=1, source_target_pairs={{8,0},{16,8},{24,16},{9,1},{17,9},{25,17},{10,2},{18,10},{26,18},{... | collective-permute-start | bytes 2555912 | tf_op jit(solution)/shard_map/while/body/eval_jaxpr/ppermute | solution.py:14
  717.7 36.4 %copy-start.9 = (f32[6656]{0:T(1024)S(1)}, f32[6656]{0:T(1024)}, u32[]{:S(2)}) copy-start(f32[6656]{0:T(1024)} %multiply_reduce_fusion.1) | copy-start | bytes 79876
  727.4 38.6 %copy-start.18 = (f32[128]{0:T(128)S(1)}, f32[128]{0:T(128)}, u32[]{:S(2)}) copy-start(f32[128]{0:T(128)} %get-tuple-element.283) | copy-start | bytes 1540
  781.6 36.7 %copy-start.1 = (bf16[512,832]{0,1:T(8,128)(2,1)S(1)}, bf16[512,832]{0,1:T(8,128)(2,1)}, u32[]{:S(2)}) copy-start(bf16[512,832]{0,1:T(8,128)(2,1)} %param.9) | copy-start | bytes 2555908
  781.7 35.4 %copy-start.13 = (f32[1,832]{1,0:T(1,128)S(1)}, f32[1,832]{1,0:T(1,128)}, u32[]{:S(2)}) copy-start(f32[1,832]{1,0:T(1,128)} %param.14) | copy-start | bytes 9988
  (29 other events, 282.1 us)
Sparse Core Ops, SparseCore 0:
  10.2 28.7 all-gather.1
  102.3 40.6 reduce-scatter.3
